TPU v7x, 32 devices: a whole 2x2x4 slice. The times are simulated.
32 devices in a mesh: axial: 8 (over y, x, core), azim: 4 (over z).
Axes of the slice: x: 2, y: 2, z: 4, core: 2. Of those that a mesh axis runs over, the one named last changes fastest.
Arguments:
- state: float32 [5, 16, 1024, 96], P(None, 'axial', 'azim'), as said below
- start: float32 [5, 16, 1024, 96], P(None, 'axial', 'azim'), as said below
- modes: int32 [64], replicated, may hold values from 1 to 512, as said below
Outputs:
- section: float32 [5, 16, 1024, 96], P(None, 'axial', 'azim')
Inputs may be any that keep to these rules, and one draw needn't show every extreme that they name: Cycle j keeps the modes 0 to modes[j] - 1; modes[j] lies between 8 * (j + 1) and 2 * 8 * (j + 1), capped at 512, which the last cycle reaches. `state`: the density (field 0) lies between 0.85 and 1.15. `start`: the density (field 0) lies between 0.85 and 1.15.
All inputs are finite; a program needn't handle non-finite values.
Results may differ from a plain program's by a relative error of at most 0.00005.
Values sent between devices are 32-bit elements; how exact they have to be, the bound alone decides.
A program may use at most 64 MiB of HBM per device.

v0:
```python
import math
import jax
import jax.numpy as jnp
from jax import lax
from jax.sharding import PartitionSpec as P

NTH = 1024
NIN = 64
GAMMA = 1.4
STEP_DT = 0.05


def swapped(value, axis, bit):
    return lax.ppermute(value, axis, [(i, i ^ 1 << bit) for i in range(lax.axis_size(axis))])


def with_halo(cells, sides, width):
    for axis, dim in sides:
        count = lax.axis_size(axis)
        head = lax.slice_in_dim(cells, 0, width, axis=dim)
        tail = lax.slice_in_dim(cells, cells.shape[dim] - width, cells.shape[dim], axis=dim)
        cells = jnp.concatenate(
            [
                lax.ppermute(tail, axis, [(i, (i + 1) % count) for i in range(count)]),
                cells,
                lax.ppermute(head, axis, [((i + 1) % count, i) for i in range(count)]),
            ],
            axis=dim,
        )
    return cells


def central_diff(values, dimension):
    length = values.shape[dimension] - 4

    def part_at(offset):
        return lax.slice_in_dim(values, offset, offset + length, axis=dimension)

    return (8.0 * (part_at(3) - part_at(1)) - (part_at(4) - part_at(0))) / 12.0


def pressure_of(values, inverse):
    kinetic = (values[1] * values[1] + values[2] * values[2] + values[3] * values[3]) * inverse
    return (GAMMA - 1.0) * (values[4] - 0.5 * kinetic)


def flux_along(values, direction):
    inverse = 1.0 / values[0]
    velocity = values[direction] * inverse
    pressure = pressure_of(values, inverse)
    components = [
        values[direction],
        values[1] * velocity,
        values[2] * velocity,
        values[3] * velocity,
        (values[4] + pressure) * velocity,
    ]
    components[direction] = components[direction] + pressure
    return jnp.stack(components)


def rates_of(padded, dtheta):
    axial_cells = padded[:, :, 2:-2, 2:-2]
    azimuth_cells = padded[:, 2:-2, :, 2:-2]
    radial_cells = padded[:, 2:-2, 2:-2, :]
    centre = padded[:, 2:-2, 2:-2, 2:-2]
    radius_all = jnp.arange(padded.shape[3], dtype=jnp.float32) - 1.5
    inv_radius = 1.0 / radius_all[2:-2]
    axial_term = central_diff(flux_along(axial_cells, 1), 1)
    radial_term = central_diff(flux_along(radial_cells, 2) * radius_all, 3) * inv_radius
    azimuth_term = central_diff(flux_along(azimuth_cells, 3), 2) * (inv_radius / dtheta)
    inverse = 1.0 / centre[0]
    pressure = pressure_of(centre, inverse)
    source_radial = (centre[3] * centre[3] * inverse + pressure) * inv_radius
    source_azimuth = -(centre[2] * centre[3] * inverse) * inv_radius
    totals = -(axial_term + radial_term + azimuth_term)
    return jnp.stack(
        [totals[0], totals[1], totals[2] + source_radial, totals[3] + source_azimuth, totals[4]]
    )


def radial_extend(haloed, partner):
    signs = jnp.array([1.0, 1.0, -1.0, -1.0, 1.0], dtype=jnp.float32).reshape(5, 1, 1, 1)
    ghost = jnp.flip(partner, 3) * signs
    rim_axial = (haloed.shape[1] - ghost.shape[1]) // 2
    rim_theta = (haloed.shape[2] - ghost.shape[2]) // 2
    ghost = jnp.pad(ghost, ((0, 0), (rim_axial, rim_axial), (rim_theta, rim_theta), (0, 0)))
    outer_cycles = jnp.repeat(haloed[..., -1:], 2, axis=3)
    return jnp.concatenate([ghost, haloed, outer_cycles], axis=3)


def fourier_tables():
    half_modes = NTH // 2
    mode_block = min(128, half_modes)
    block_count = half_modes // mode_block
    wavenumbers = jnp.arange(half_modes, dtype=jnp.int32)
    cell_numbers = jnp.arange(NTH, dtype=jnp.int32)
    phase_index = cell_numbers[:, None] * wavenumbers[None, :] % NTH
    angles = phase_index.astype(jnp.float32) * (2.0 * math.pi / NTH)
    cosines = jnp.cos(angles).reshape(NTH, block_count, mode_block).transpose(1, 0, 2)
    sines = jnp.sin(angles).reshape(NTH, block_count, mode_block).transpose(1, 0, 2)
    tables = jnp.concatenate([cosines, sines], axis=2)
    weights = (
        jnp.where(wavenumbers == 0, 1.0 / NTH, 2.0 / NTH)
        .astype(jnp.float32)
        .reshape(block_count, mode_block)
    )
    return (tables, weights, wavenumbers.reshape(block_count, mode_block), mode_block)


def truncate_cycles(slab, local_modes, tables, weights, wave_blocks, mode_block):

    def one_cycle(cycle_index, result):
        cycle_values = lax.dynamic_index_in_dim(slab, cycle_index, 1, keepdims=False)
        mode_count = lax.dynamic_index_in_dim(local_modes, cycle_index, 0, keepdims=False)
        used_blocks = (mode_count + mode_block - 1) // mode_block

        def one_block(block_index, series_sum):
            basis_block = lax.dynamic_index_in_dim(tables, block_index, 0, keepdims=False)
            coeffs = jnp.dot(cycle_values, basis_block, precision=lax.Precision.HIGHEST)
            block_waves = lax.dynamic_index_in_dim(wave_blocks, block_index, 0, keepdims=False)
            block_weights = lax.dynamic_index_in_dim(weights, block_index, 0, keepdims=False)
            kept_weights = jnp.where(block_waves < mode_count, block_weights, 0.0)
            scaled = coeffs * jnp.concatenate([kept_weights, kept_weights])
            return series_sum + lax.dot_general(
                scaled, basis_block, (((1,), (1,)), ((), ())), precision=lax.Precision.HIGHEST
            )

        series = lax.fori_loop(
            0, used_blocks, one_block, jnp.zeros(cycle_values.shape, jnp.float32)
        )
        return lax.dynamic_update_index_in_dim(result, series, cycle_index, 1)

    return lax.fori_loop(0, slab.shape[1], one_cycle, jnp.zeros(slab.shape, jnp.float32))


def shards(state, start, modes):
    field_count, axial_local, theta_local, cycle_total = state.shape
    azim_size = lax.axis_size("azim")
    azim_index = lax.axis_index("azim")
    cycles_local = NIN // azim_size
    item_count = field_count * axial_local
    tables, weights, wave_blocks, mode_block = fourier_tables()
    inner = state[..., :NIN].transpose(0, 1, 3, 2).reshape(item_count, NIN, theta_local)
    local_modes = lax.dynamic_slice_in_dim(modes, azim_index * cycles_local, cycles_local)
    smoothed = truncate_cycles(
        lax.all_to_all(inner, "azim", split_axis=1, concat_axis=2, tiled=True),
        local_modes,
        tables,
        weights,
        wave_blocks,
        mode_block,
    )
    exchanged = lax.all_to_all(smoothed, "azim", split_axis=2, concat_axis=1, tiled=True)
    smooth_inner = exchanged.reshape(field_count, axial_local, NIN, theta_local).transpose(
        0, 1, 3, 2
    )
    smoothed_state = jnp.concatenate([smooth_inner, state[..., NIN:]], axis=3)
    partner = swapped(smoothed_state[..., :2], "azim", azim_size.bit_length() - 2)
    haloed = with_halo(smoothed_state, (("axial", 1), ("azim", 2)), 2)
    padded = radial_extend(haloed, partner)
    rate = rates_of(padded, 2.0 * math.pi / NTH)
    return start + STEP_DT * rate


def solution(mesh):
    in_specs = (P(None, "axial", "azim", None), P(None, "axial", "azim", None), P())
    out_specs = P(None, "axial", "azim", None)
    return jax.shard_map(shards, mesh=mesh, in_specs=in_specs, out_specs=out_specs, check_vma=False)
```

profile of v0, /device:TPU:0, one launch (start us, length us, event | category | flops | bytes accessed | tf_op | source)
XLA Modules:
  0.0 475.3 jit_solution(14893907723052022930)
XLA Ops:
  2.6 6.3 %all-to-all-start = ((f32[10,64,256]{2,0,1:T(8,128)}), f32[10,64,256]{2,0,1:T(8,128)S(1)}, u32[]{:S(2)}, u32[]{:S(2)}) async-start(f32[10,64,256]{2,0,1:T(8,128)} %copy.27), calls=%async_computation | async-start | bytes 2097152 | tf_op jit(solution)/shard_map/all_to_all | solution.py:147
  9.0 8.1 %fusion.19 = (f32[4,1024,128]{2,1,0:T(8,128)S(1)}, f32[4,1024,128]{2,1,0:T(8,128)S(1)}) fusion(s32[4,128]{1,0:T(4,128)S(1)} %multiply_add_fusion.1), kind=kLoop, calls=%fused_computation.45 | loop fusion | flops 7340032 | bytes 4196352 | tf_op jit(solution)/shard_map/cos | solution.py:100
  19.4 15.3 %all-to-all-done = f32[10,64,256]{2,0,1:T(8,128)S(1)} async-done(((f32[10,64,256]{2,0,1:T(8,128)}), f32[10,64,256]{2,0,1:T(8,128)S(1)}, u32[]{:S(2)}, u32[]{:S(2)}) %all-to-all-start) | async-done | bytes 655392 | tf_op jit(solution)/shard_map/all_to_all | solution.py:147
  35.4 122.0 %while.64 = (s32[]{:T(128)}, f32[10,16,1024]{2,0,1:T(8,128)}, s32[16]{0:T(128)S(1)}, f32[10,16,1024]{2,0,1:T(8,128)S(1)}, f32[4,1024,256]{2,1,0:T(8,128)}, /*ind...) while((s32[]{:T(128)}, f32[10,16,1024]{2,0,1:T(8,128)}, ...), condition=%wide.region_3.4_spmd.clone, body=%wide.region_0.3_spmd.clone.sunk | while | flops 62930964 | bytes 2478670 | solution.py:134
  36.6 4.6 while.65
  43.1 4.6 while.65
  49.6 4.6 while.65
  62.5 4.6 while.65
  69.0 4.6 while.65
  75.4 4.6 while.65
  81.9 4.6 while.65
  107.8 9.3 %while.65 = (s32[]{:T(128)}, f32[10,1024]{1,0:T(8,128)S(1)}, s32[]{:T(128)}, f32[4,1024,256]{2,1,0:T(8,128)}, f32[10,1024]{1,0:T(8,128)S(1)}, /*index=5*/s32[4,1...) while((s32[]{:T(128)}, f32[10,1024]{1,0:T(8,128)S(1)}, ...), condition=%wide.region_2.2_spmd, body=%wide.region_1.1_spmd.sunk | while | flops 62927876 | bytes 2244775 | solution.py:129
  118.9 9.3 %while.65 = (s32[]{:T(128)}, f32[10,1024]{1,0:T(8,128)S(1)}, s32[]{:T(128)}, f32[4,1024,256]{2,1,0:T(8,128)}, f32[10,1024]{1,0:T(8,128)S(1)}, /*index=5*/s32[4,1...) while((s32[]{:T(128)}, f32[10,1024]{1,0:T(8,128)S(1)}, ...), condition=%wide.region_2.2_spmd, body=%wide.region_1.1_spmd.sunk | while | flops 62927876 | bytes 2244775 | solution.py:129
  136.4 9.3 %while.65 = (s32[]{:T(128)}, f32[10,1024]{1,0:T(8,128)S(1)}, s32[]{:T(128)}, f32[4,1024,256]{2,1,0:T(8,128)}, f32[10,1024]{1,0:T(8,128)S(1)}, /*index=5*/s32[4,1...) while((s32[]{:T(128)}, f32[10,1024]{1,0:T(8,128)S(1)}, ...), condition=%wide.region_2.2_spmd, body=%wide.region_1.1_spmd.sunk | while | flops 62927876 | bytes 2244775 | solution.py:129
  147.5 9.3 %while.65 = (s32[]{:T(128)}, f32[10,1024]{1,0:T(8,128)S(1)}, s32[]{:T(128)}, f32[4,1024,256]{2,1,0:T(8,128)}, f32[10,1024]{1,0:T(8,128)S(1)}, /*index=5*/s32[4,1...) while((s32[]{:T(128)}, f32[10,1024]{1,0:T(8,128)S(1)}, ...), condition=%wide.region_2.2_spmd, body=%wide.region_1.1_spmd.sunk | while | flops 62927876 | bytes 2244775 | solution.py:129
  157.5 7.1 %copy.31 = f32[10,16,1024]{0,1,2:T(8,128)} copy(f32[10,16,1024]{2,0,1:T(8,128)} %get-tuple-element.299) | data formatting | bytes 1310720 | tf_op jit(solution)/shard_map/while | solution.py:134
  164.6 9.5 %reshape.52 = f32[4,1,40960]{2,1,0:T(1,128)} reshape(f32[1024,16,10]{2,1,0:T(8,128)} %bitcast.58) | data formatting | bytes 1310720
  174.0 206.8 %all-to-all-start.1 = ((f32[4,1,40960]{2,1,0:T(1,128)}), f32[4,1,40960]{2,1,0:T(1,128)S(1)}, u32[]{:S(2)}, u32[]{:S(2)}) async-start(f32[4,1,40960]{2,1,0:T(1,128)} %reshape.52), calls=%async_computation.1 | async-start | bytes 1310720 | tf_op jit(solution)/shard_map/all_to_all | solution.py:154
  381.9 15.2 %all-to-all-done.1 = f32[4,1,40960]{2,1,0:T(1,128)S(1)} async-done(((f32[4,1,40960]{2,1,0:T(1,128)}), f32[4,1,40960]{2,1,0:T(1,128)S(1)}, u32[]{:S(2)}, u32[]{:S(2)}) %all-to-all-start.1) | async-done | bytes 655392 | tf_op jit(solution)/shard_map/all_to_all | solution.py:154
  400.1 12.5 %reshape.53 = f32[1024,16,10]{2,1,0:T(8,128)} reshape(f32[4,40960]{1,0:T(4,128)S(1)} %reduce) | data formatting | bytes 1310720
  412.6 5.4 %copy.40 = f32[10,16,4,256]{3,2,1,0:T(4,128)S(1)} copy(f32[10,16,4,256]{0,1,3,2:T(8,128)} %bitcast.59) | data formatting | bytes 1310720 | tf_op jit(solution)/shard_map/all_to_all | solution.py:154
  420.6 4.7 collective-permute-done.2
  425.5 17.2 %collective-permute-done.1 = f32[5,2,256,96]{2,3,1,0:T(8,128)S(1)} collective-permute-done((f32[5,2,256,96]{2,3,1,0:T(8,128)}, f32[5,2,256,96]{2,3,1,0:T(8,128)S(1)}, u32[]{:S(2)}, u32[]{:S(2)}) %collective-permute-start.1) | collective-permute-done | bytes 983072 | tf_op jit(solution)/shard_map/ppermute | solution.py:26
  462.4 6.0 %fusion.11 = f32[5,6,260,100]{2,3,1,0:T(8,128)S(1)} fusion(f32[5,2,256,2]{2,3,1,0:T(2,128)S(1)} %broadcast_multiply_fusion.1, f32[5,6,260,2]{2,3,1,0:T(2,128)S(1)} %reshape.50, f32[5,6,2,96]{2,3,1,0:T(8,128)S(1)} %copy.37, f32[5,2,256,96]{2,3,1,0:T(8,128)S(1)} %copy-done.3, f32[5,2,256,32]{2,3,1,0:T(8,128)S(1)} %slice.186, ...), kind=kLoop, calls=%fused_computation.20 | loop fusion | flops 7020000 | bytes 6198080 | tf_op jit(solution)/shard_map/concatenate | solution.py:89
  (261 shorter events, 173.2 us)
Async XLA Ops:
  1.1 7.8 %copy-start.11 = (s32[64]{0:T(128)S(1)}, s32[64]{0:T(128)}, u32[]{:S(2)}) copy-start(s32[64]{0:T(128)} %param.10) | copy-start | bytes 772
  2.6 32.1 %all-to-all-start = ((f32[10,64,256]{2,0,1:T(8,128)}), f32[10,64,256]{2,0,1:T(8,128)S(1)}, u32[]{:S(2)}, u32[]{:S(2)}) async-start(f32[10,64,256]{2,0,1:T(8,128)} %copy.27), calls=%async_computation | async-start | bytes 2097152 | tf_op jit(solution)/shard_map/all_to_all | solution.py:147
  174.0 223.0 %all-to-all-start.1 = ((f32[4,1,40960]{2,1,0:T(1,128)}), f32[4,1,40960]{2,1,0:T(1,128)S(1)}, u32[]{:S(2)}, u32[]{:S(2)}) async-start(f32[4,1,40960]{2,1,0:T(1,128)} %reshape.52), calls=%async_computation.1 | async-start | bytes 1310720 | tf_op jit(solution)/shard_map/all_to_all | solution.py:154
  418.0 7.4 %copy-start.10 = (f32[5]{0:T(128)S(1)}, f32[5]{0:T(128)}, u32[]{:S(2)}) copy-start(f32[5]{0:T(128)} %constant.217.clone) | copy-start | bytes 64
  418.1 26.6 %copy-start = (f32[10,4,16,256]{3,2,1,0:T(8,128)}, f32[10,4,16,256]{3,2,1,0:T(8,128)S(1)}, u32[]{:S(2)}) copy-start(f32[10,4,16,256]{3,2,1,0:T(8,128)S(1)} %copy.33) | copy-start | bytes 1966084
  419.3 23.4 %collective-permute-start.1 = (f32[5,2,256,96]{2,3,1,0:T(8,128)}, f32[5,2,256,96]{2,3,1,0:T(8,128)S(1)}, u32[]{:S(2)}, u32[]{:S(2)}) collective-permute-start(f32[5,2,256,96]{2,3,1,0:T(8,128)} %pad_maximum_fusion.3), channel_id=1, source_target_pairs={{4,0},{8,4},{12,8},{16,12},{20,16},{24,20},{28,24},{0,28},{5,1},{9... | collective-permute-start | bytes 2949128 | tf_op jit(solution)/shard_map/ppermute | solution.py:26
  420.4 24.1 %collective-permute-start = (f32[5,2,256,96]{2,3,1,0:T(8,128)}, f32[5,2,256,96]{2,3,1,0:T(8,128)S(1)}, u32[]{:S(2)}, u32[]{:S(2)}) collective-permute-start(f32[5,2,256,96]{2,3,1,0:T(8,128)} %pad_maximum_fusion.3), channel_id=1, source_target_pairs={{0,4},{4,8},{8,12},{12,16},{16,20},{20,24},{24,28},{28,0},{1,5},{5... | collective-permute-start | bytes 2949128 | tf_op jit(solution)/shard_map/ppermute | solution.py:24
  420.5 4.7 collective-permute-start.2
  442.7 2.1 copy-start.2
  444.5 0.9 copy-start.4
  445.5 2.5 copy-start.6
  448.9 6.1 %copy-start.7 = (f32[5,6,256,96]{2,3,1,0:T(8,128)S(1)}, f32[5,6,256,96]{2,3,1,0:T(8,128)}, u32[]{:S(2)}) copy-start(f32[5,6,256,96]{2,3,1,0:T(8,128)} %copy-done.6) | copy-start | bytes 8847364
  450.8 8.0 %collective-permute-start.4 = (f32[5,6,2,96]{3,2,1,0:T(2,128)S(1)}, f32[5,6,2,96]{3,2,1,0:T(2,128)S(1)}, u32[]{:S(2)}, u32[]{:S(2)}) collective-permute-start(f32[5,6,2,96]{3,2,1,0:T(2,128)S(1)} %copy.35), channel_id=1, source_target_pairs={{1,0},{2,1},{3,2},{0,3},{5,4},{6,5},{7,6},{4,7},{9,8},{10,9},{11,1... | collective-permute-start | bytes 69128 | tf_op jit(solution)/shard_map/ppermute | solution.py:26
  454.2 5.9 %collective-permute-start.3 = (f32[5,6,2,96]{3,2,1,0:T(2,128)S(1)}, f32[5,6,2,96]{3,2,1,0:T(2,128)S(1)}, u32[]{:S(2)}, u32[]{:S(2)}) collective-permute-start(f32[5,6,2,96]{3,2,1,0:T(2,128)S(1)} %copy.34), channel_id=1, source_target_pairs={{0,1},{1,2},{2,3},{3,0},{4,5},{5,6},{6,7},{7,4},{8,9},{9,10},{10,1... | collective-permute-start | bytes 69128 | tf_op jit(solution)/shard_map/ppermute | solution.py:24
  460.6 1.4 copy-start.1
  460.6 1.5 copy-start.3
  460.6 1.8 copy-start.5
  470.2 1.8 copy-start.8
  473.0 1.2 copy-start.9
where the time goes:
time: 481 us; the launch traced here: 475 us
  starting transfers between devices  217 us (45%)
  matrix products  80.6 us (17%)
  local copies, waits for them, and re-layouts  70.8 us (15%)
  waiting for transfers between devices  54.9 us (11%)
  other arithmetic  41 us (9%)
  loops' own time  10.8 us (2%)
    all_to_all x1, starting transfers between devices, shards(): lax.all_to_all(smoothed, 'azim', split_axis=2, concat_axis=1, tiled=True)  207 us
    dot_general x20, matrix products, one_block(): lax.dot_general(scaled, basis_block, (((1,), (1,)), ((), ())), precision=...  43.9 us
    dot_general x20, matrix products, one_block(): coeffs = jnp.dot(cycle_values, basis_block, precision=lax.Precision.HIGHEST)  36.7 us
    unnamed x31, local copies, waits for them, and re-layouts  27.4 us
    ppermute x2, waiting for transfers between devices, with_halo(): lax.ppermute(head, axis, [((i + 1) % count, i) for i in range(count)])  17.2 us
    all_to_all x1, waiting for transfers between devices, shards(): lax.all_to_all(inner, 'azim', split_axis=1, concat_axis=2, tiled=True)  15.3 us
    all_to_all x1, waiting for transfers between devices, shards(): lax.all_to_all(smoothed, 'azim', split_axis=2, concat_axis=1, tiled=True)  15.2 us
    select_n x20, other arithmetic, one_block(): kept_weights = jnp.where(block_waves < mode_count, block_weights, 0.0)  11.1 us
  transfers between devices with their start and end apart: 7, of which 6 were waited for; matrix products, arithmetic and copies ran while one was open for 4% of the time, Pallas kernels for 0%

commit v1 on v0

--- a/solution.py
+++ b/solution.py
@@ -151,7 +151,10 @@
         wave_blocks,
         mode_block,
     )
-    exchanged = lax.all_to_all(smoothed, "azim", split_axis=2, concat_axis=1, tiled=True)
+    size = lax.axis_size("azim")
+    shards_2 = jnp.stack(jnp.split(smoothed, size, axis=2), axis=0)
+    shards_2 = lax.all_to_all(shards_2, "azim", split_axis=0, concat_axis=0)
+    exchanged = jnp.concatenate(shards_2, axis=1)
     smooth_inner = exchanged.reshape(field_count, axial_local, NIN, theta_local).transpose(
         0, 1, 3, 2
     )

time: 481 us -> 445 us (0.925)
  local copies, waits for them, and re-layouts: 70.8 us -> 34.8 us
    unnamed x31 -> x29, local copies, waits for them, and re-layouts: 27.4 us -> 5.49 us
    while x1 -> x0, local copies, waits for them, and re-layouts: 7.12 us -> none  [truncate_cycles(): lax.fori_loop(0, slab.shape[1], one_cycle, jnp.zeros(slab.shape, jnp.floa...]
    all_to_all x3 -> x1, local copies, waits for them, and re-layouts: 6.03 us -> 0.05 us  [shards(): shards_2 = lax.all_to_all(shards_2, 'azim', split_axis=0, concat_axis=0)]
    dynamic_update_slice x16 -> x32, local copies, waits for them, and re-layouts: 10 us -> 8.49 us  [one_cycle(): return lax.dynamic_update_index_in_dim(result, series, cycle_index, 1)]
where the time goes in v1:
time: 445 us; the launch traced here: 439 us
  starting transfers between devices  217 us (49%)
  matrix products  80.6 us (18%)
  waiting for transfers between devices  54.9 us (12%)
  other arithmetic  39.7 us (9%)
  local copies, waits for them, and re-layouts  34.8 us (8%)
  loops' own time  11.5 us (3%)
    all_to_all x1, starting transfers between devices, shards(): shards_2 = lax.all_to_all(shards_2, 'azim', split_axis=0, concat_axis=0)  208 us
    dot_general x20, matrix products, one_block(): lax.dot_general(scaled, basis_block, (((1,), (1,)), ((), ())), precision=...  43.9 us
    dot_general x20, matrix products, one_block(): coeffs = jnp.dot(cycle_values, basis_block, precision=lax.Precision.HIGHEST)  36.7 us
    ppermute x2, waiting for transfers between devices, with_halo(): lax.ppermute(head, axis, [((i + 1) % count, i) for i in range(count)])  17.2 us
    all_to_all x1, waiting for transfers between devices, shards(): lax.all_to_all(inner, 'azim', split_axis=1, concat_axis=2, tiled=True)  15.3 us
    all_to_all x1, waiting for transfers between devices, shards(): shards_2 = lax.all_to_all(shards_2, 'azim', split_axis=0, concat_axis=0)  15.1 us
    select_n x20, other arithmetic, one_block(): kept_weights = jnp.where(block_waves < mode_count, block_weights, 0.0)  11.4 us
    another operation x1, loops' own time, truncate_cycles(): lax.fori_loop(0, slab.shape[1], one_cycle, jnp.zeros(slab.shape, jnp.floa...  10.5 us
  transfers between devices with their start and end apart: 7, of which 6 were waited for; matrix products, arithmetic and copies ran while one was open for 4% of the time, Pallas kernels for 0%

profile of v1, /device:TPU:0, one launch (start us, length us, event | category | flops | bytes accessed | tf_op | source)
XLA Modules:
  0.0 439.0 jit_solution(7469195461948029456)
XLA Ops:
  2.6 6.3 %all-to-all-start = ((f32[10,64,256]{2,0,1:T(8,128)}), f32[10,64,256]{2,0,1:T(8,128)S(1)}, u32[]{:S(2)}, u32[]{:S(2)}) async-start(f32[10,64,256]{2,0,1:T(8,128)} %copy.30), calls=%async_computation | async-start | bytes 2097152 | tf_op jit(solution)/shard_map/all_to_all | solution.py:147
  9.0 8.1 %fusion.19 = (f32[4,1024,128]{2,1,0:T(8,128)S(1)}, f32[4,1024,128]{2,1,0:T(8,128)S(1)}) fusion(s32[4,128]{1,0:T(4,128)S(1)} %multiply_add_fusion.1), kind=kLoop, calls=%fused_computation.44 | loop fusion | flops 7340032 | bytes 4196352 | tf_op jit(solution)/shard_map/cos | solution.py:100
  19.4 15.3 %all-to-all-done = f32[10,64,256]{2,0,1:T(8,128)S(1)} async-done(((f32[10,64,256]{2,0,1:T(8,128)}), f32[10,64,256]{2,0,1:T(8,128)S(1)}, u32[]{:S(2)}, u32[]{:S(2)}) %all-to-all-start) | async-done | bytes 655392 | tf_op jit(solution)/shard_map/all_to_all | solution.py:147
  35.5 122.0 %while.64 = (s32[]{:T(128)}, f32[10,16,1024]{2,1,0:T(8,128)S(1)}, s32[16]{0:T(128)S(1)}, f32[10,16,1024]{2,0,1:T(8,128)S(1)}, f32[4,1024,256]{2,1,0:T(8,128)}, /...) while((s32[]{:T(128)}, f32[10,16,1024]{2,1,0:T(8,128)S(1)}, ...), condition=%wide.region_3.4_spmd.clone, body=%wide.region_0.3_spmd.clone.sunk | while | flops 62930964 | bytes 2536014 | solution.py:134
  36.7 4.7 %while.65 = (s32[]{:T(128)}, f32[10,1024]{1,0:T(8,128)S(1)}, s32[]{:T(128)}, f32[4,1024,256]{2,1,0:T(8,128)}, f32[10,1024]{1,0:T(8,128)S(1)}, /*index=5*/s32[4,1...) while((s32[]{:T(128)}, f32[10,1024]{1,0:T(8,128)S(1)}, ...), condition=%wide.region_2.2_spmd, body=%wide.region_1.1_spmd.sunk | while | flops 62927876 | bytes 2244775 | solution.py:129
  43.2 4.7 %while.65 = (s32[]{:T(128)}, f32[10,1024]{1,0:T(8,128)S(1)}, s32[]{:T(128)}, f32[4,1024,256]{2,1,0:T(8,128)}, f32[10,1024]{1,0:T(8,128)S(1)}, /*index=5*/s32[4,1...) while((s32[]{:T(128)}, f32[10,1024]{1,0:T(8,128)S(1)}, ...), condition=%wide.region_2.2_spmd, body=%wide.region_1.1_spmd.sunk | while | flops 62927876 | bytes 2244775 | solution.py:129
  49.6 4.7 %while.65 = (s32[]{:T(128)}, f32[10,1024]{1,0:T(8,128)S(1)}, s32[]{:T(128)}, f32[4,1024,256]{2,1,0:T(8,128)}, f32[10,1024]{1,0:T(8,128)S(1)}, /*index=5*/s32[4,1...) while((s32[]{:T(128)}, f32[10,1024]{1,0:T(8,128)S(1)}, ...), condition=%wide.region_2.2_spmd, body=%wide.region_1.1_spmd.sunk | while | flops 62927876 | bytes 2244775 | solution.py:129
  56.1 4.7 %while.65 = (s32[]{:T(128)}, f32[10,1024]{1,0:T(8,128)S(1)}, s32[]{:T(128)}, f32[4,1024,256]{2,1,0:T(8,128)}, f32[10,1024]{1,0:T(8,128)S(1)}, /*index=5*/s32[4,1...) while((s32[]{:T(128)}, f32[10,1024]{1,0:T(8,128)S(1)}, ...), condition=%wide.region_2.2_spmd, body=%wide.region_1.1_spmd.sunk | while | flops 62927876 | bytes 2244775 | solution.py:129
  62.5 4.7 %while.65 = (s32[]{:T(128)}, f32[10,1024]{1,0:T(8,128)S(1)}, s32[]{:T(128)}, f32[4,1024,256]{2,1,0:T(8,128)}, f32[10,1024]{1,0:T(8,128)S(1)}, /*index=5*/s32[4,1...) while((s32[]{:T(128)}, f32[10,1024]{1,0:T(8,128)S(1)}, ...), condition=%wide.region_2.2_spmd, body=%wide.region_1.1_spmd.sunk | while | flops 62927876 | bytes 2244775 | solution.py:129
  69.0 4.7 %while.65 = (s32[]{:T(128)}, f32[10,1024]{1,0:T(8,128)S(1)}, s32[]{:T(128)}, f32[4,1024,256]{2,1,0:T(8,128)}, f32[10,1024]{1,0:T(8,128)S(1)}, /*index=5*/s32[4,1...) while((s32[]{:T(128)}, f32[10,1024]{1,0:T(8,128)S(1)}, ...), condition=%wide.region_2.2_spmd, body=%wide.region_1.1_spmd.sunk | while | flops 62927876 | bytes 2244775 | solution.py:129
  75.5 4.7 %while.65 = (s32[]{:T(128)}, f32[10,1024]{1,0:T(8,128)S(1)}, s32[]{:T(128)}, f32[4,1024,256]{2,1,0:T(8,128)}, f32[10,1024]{1,0:T(8,128)S(1)}, /*index=5*/s32[4,1...) while((s32[]{:T(128)}, f32[10,1024]{1,0:T(8,128)S(1)}, ...), condition=%wide.region_2.2_spmd, body=%wide.region_1.1_spmd.sunk | while | flops 62927876 | bytes 2244775 | solution.py:129
  81.9 4.7 %while.65 = (s32[]{:T(128)}, f32[10,1024]{1,0:T(8,128)S(1)}, s32[]{:T(128)}, f32[4,1024,256]{2,1,0:T(8,128)}, f32[10,1024]{1,0:T(8,128)S(1)}, /*index=5*/s32[4,1...) while((s32[]{:T(128)}, f32[10,1024]{1,0:T(8,128)S(1)}, ...), condition=%wide.region_2.2_spmd, body=%wide.region_1.1_spmd.sunk | while | flops 62927876 | bytes 2244775 | solution.py:129
  88.4 4.7 %while.65 = (s32[]{:T(128)}, f32[10,1024]{1,0:T(8,128)S(1)}, s32[]{:T(128)}, f32[4,1024,256]{2,1,0:T(8,128)}, f32[10,1024]{1,0:T(8,128)S(1)}, /*index=5*/s32[4,1...) while((s32[]{:T(128)}, f32[10,1024]{1,0:T(8,128)S(1)}, ...), condition=%wide.region_2.2_spmd, body=%wide.region_1.1_spmd.sunk | while | flops 62927876 | bytes 2244775 | solution.py:129
  94.8 4.7 %while.65 = (s32[]{:T(128)}, f32[10,1024]{1,0:T(8,128)S(1)}, s32[]{:T(128)}, f32[4,1024,256]{2,1,0:T(8,128)}, f32[10,1024]{1,0:T(8,128)S(1)}, /*index=5*/s32[4,1...) while((s32[]{:T(128)}, f32[10,1024]{1,0:T(8,128)S(1)}, ...), condition=%wide.region_2.2_spmd, body=%wide.region_1.1_spmd.sunk | while | flops 62927876 | bytes 2244775 | solution.py:129
  101.3 4.7 %while.65 = (s32[]{:T(128)}, f32[10,1024]{1,0:T(8,128)S(1)}, s32[]{:T(128)}, f32[4,1024,256]{2,1,0:T(8,128)}, f32[10,1024]{1,0:T(8,128)S(1)}, /*index=5*/s32[4,1...) while((s32[]{:T(128)}, f32[10,1024]{1,0:T(8,128)S(1)}, ...), condition=%wide.region_2.2_spmd, body=%wide.region_1.1_spmd.sunk | while | flops 62927876 | bytes 2244775 | solution.py:129
  107.7 9.3 %while.65 = (s32[]{:T(128)}, f32[10,1024]{1,0:T(8,128)S(1)}, s32[]{:T(128)}, f32[4,1024,256]{2,1,0:T(8,128)}, f32[10,1024]{1,0:T(8,128)S(1)}, /*index=5*/s32[4,1...) while((s32[]{:T(128)}, f32[10,1024]{1,0:T(8,128)S(1)}, ...), condition=%wide.region_2.2_spmd, body=%wide.region_1.1_spmd.sunk | while | flops 62927876 | bytes 2244775 | solution.py:129
  118.9 9.3 %while.65 = (s32[]{:T(128)}, f32[10,1024]{1,0:T(8,128)S(1)}, s32[]{:T(128)}, f32[4,1024,256]{2,1,0:T(8,128)}, f32[10,1024]{1,0:T(8,128)S(1)}, /*index=5*/s32[4,1...) while((s32[]{:T(128)}, f32[10,1024]{1,0:T(8,128)S(1)}, ...), condition=%wide.region_2.2_spmd, body=%wide.region_1.1_spmd.sunk | while | flops 62927876 | bytes 2244775 | solution.py:129
  130.0 4.7 %while.65 = (s32[]{:T(128)}, f32[10,1024]{1,0:T(8,128)S(1)}, s32[]{:T(128)}, f32[4,1024,256]{2,1,0:T(8,128)}, f32[10,1024]{1,0:T(8,128)S(1)}, /*index=5*/s32[4,1...) while((s32[]{:T(128)}, f32[10,1024]{1,0:T(8,128)S(1)}, ...), condition=%wide.region_2.2_spmd, body=%wide.region_1.1_spmd.sunk | while | flops 62927876 | bytes 2244775 | solution.py:129
  136.4 9.3 %while.65 = (s32[]{:T(128)}, f32[10,1024]{1,0:T(8,128)S(1)}, s32[]{:T(128)}, f32[4,1024,256]{2,1,0:T(8,128)}, f32[10,1024]{1,0:T(8,128)S(1)}, /*index=5*/s32[4,1...) while((s32[]{:T(128)}, f32[10,1024]{1,0:T(8,128)S(1)}, ...), condition=%wide.region_2.2_spmd, body=%wide.region_1.1_spmd.sunk | while | flops 62927876 | bytes 2244775 | solution.py:129
  147.5 9.3 %while.65 = (s32[]{:T(128)}, f32[10,1024]{1,0:T(8,128)S(1)}, s32[]{:T(128)}, f32[4,1024,256]{2,1,0:T(8,128)}, f32[10,1024]{1,0:T(8,128)S(1)}, /*index=5*/s32[4,1...) while((s32[]{:T(128)}, f32[10,1024]{1,0:T(8,128)S(1)}, ...), condition=%wide.region_2.2_spmd, body=%wide.region_1.1_spmd.sunk | while | flops 62927876 | bytes 2244775 | solution.py:129
  158.4 207.5 %all-to-all-start.1 = ((f32[4,10,16,256]{3,2,1,0:T(8,128)}), f32[4,10,16,256]{3,2,1,0:T(8,128)S(1)}, u32[]{:S(2)}, u32[]{:S(2)}) async-start(f32[4,10,16,256]{3,2,1,0:T(8,128)} %pad_maximum_fusion.4), calls=%async_computation.1 | async-start | bytes 1310720 | tf_op jit(solution)/shard_map/all_to_all | solution.py:156
  366.9 15.1 %all-to-all-done.1 = f32[4,10,16,256]{3,2,1,0:T(8,128)S(1)} async-done(((f32[4,10,16,256]{3,2,1,0:T(8,128)}), f32[4,10,16,256]{3,2,1,0:T(8,128)S(1)}, u32[]{:S(2)}, u32[]{:S(2)}) %all-to-all-start.1) | async-done | bytes 655392 | tf_op jit(solution)/shard_map/all_to_all | solution.py:156
  389.5 17.2 %collective-permute-done.1 = f32[5,2,256,96]{2,3,1,0:T(8,128)S(1)} collective-permute-done((f32[5,2,256,96]{2,3,1,0:T(8,128)}, f32[5,2,256,96]{2,3,1,0:T(8,128)S(1)}, u32[]{:S(2)}, u32[]{:S(2)}) %collective-permute-start.1) | collective-permute-done | bytes 983072 | tf_op jit(solution)/shard_map/ppermute | solution.py:26
  426.2 6.0 %fusion.11 = f32[5,6,260,100]{2,3,1,0:T(8,128)S(1)} fusion(f32[5,2,256,2]{2,3,1,0:T(2,128)S(1)} %broadcast_multiply_fusion.1, f32[5,6,260,2]{2,3,1,0:T(2,128)S(1)} %reshape.49, f32[5,6,2,96]{2,3,1,0:T(8,128)S(1)} %copy.42, f32[5,2,256,96]{2,3,1,0:T(8,128)S(1)} %copy-done.3, f32[5,2,256,32]{2,3,1,0:T(8,128)S(1)} %slice.186, ...), kind=kLoop, calls=%fused_computation.19 | loop fusion | flops 7020000 | bytes 6198080 | tf_op jit(solution)/shard_map/concatenate | solution.py:89
  (273 shorter events, 151.6 us)
Async XLA Ops:
  1.1 7.8 %copy-start.11 = (s32[64]{0:T(128)S(1)}, s32[64]{0:T(128)}, u32[]{:S(2)}) copy-start(s32[64]{0:T(128)} %param.10) | copy-start | bytes 772
  2.6 32.1 %all-to-all-start = ((f32[10,64,256]{2,0,1:T(8,128)}), f32[10,64,256]{2,0,1:T(8,128)S(1)}, u32[]{:S(2)}, u32[]{:S(2)}) async-start(f32[10,64,256]{2,0,1:T(8,128)} %copy.30), calls=%async_computation | async-start | bytes 2097152 | tf_op jit(solution)/shard_map/all_to_all | solution.py:147
  158.4 223.7 %all-to-all-start.1 = ((f32[4,10,16,256]{3,2,1,0:T(8,128)}), f32[4,10,16,256]{3,2,1,0:T(8,128)S(1)}, u32[]{:S(2)}, u32[]{:S(2)}) async-start(f32[4,10,16,256]{3,2,1,0:T(8,128)} %pad_maximum_fusion.4), calls=%async_computation.1 | async-start | bytes 1310720 | tf_op jit(solution)/shard_map/all_to_all | solution.py:156
  365.9 23.5 %copy-start.10 = (f32[5]{0:T(128)S(1)}, f32[5]{0:T(128)}, u32[]{:S(2)}) copy-start(f32[5]{0:T(128)} %constant.217.clone) | copy-start | bytes 64
  382.1 26.6 %copy-start = (f32[4,10,16,256]{3,2,0,1:T(8,128)}, f32[4,10,16,256]{3,2,0,1:T(8,128)S(1)}, u32[]{:S(2)}) copy-start(f32[4,10,16,256]{3,2,0,1:T(8,128)S(1)} %copy.38) | copy-start | bytes 1966084
  383.3 23.4 %collective-permute-start.1 = (f32[5,2,256,96]{2,3,1,0:T(8,128)}, f32[5,2,256,96]{2,3,1,0:T(8,128)S(1)}, u32[]{:S(2)}, u32[]{:S(2)}) collective-permute-start(f32[5,2,256,96]{2,3,1,0:T(8,128)} %pad_maximum_fusion.3), channel_id=1, source_target_pairs={{4,0},{8,4},{12,8},{16,12},{20,16},{24,20},{28,24},{0,28},{5,1},{9... | collective-permute-start | bytes 2949128 | tf_op jit(solution)/shard_map/ppermute | solution.py:26
  384.5 24.1 %collective-permute-start = (f32[5,2,256,96]{2,3,1,0:T(8,128)}, f32[5,2,256,96]{2,3,1,0:T(8,128)S(1)}, u32[]{:S(2)}, u32[]{:S(2)}) collective-permute-start(f32[5,2,256,96]{2,3,1,0:T(8,128)} %pad_maximum_fusion.3), channel_id=1, source_target_pairs={{0,4},{4,8},{8,12},{12,16},{16,20},{20,24},{24,28},{28,0},{1,5},{5... | collective-permute-start | bytes 2949128 | tf_op jit(solution)/shard_map/ppermute | solution.py:24
  384.5 4.7 %collective-permute-start.2 = (f32[5,2,256,2]{2,3,1,0:T(2,128)S(1)}, f32[5,2,256,2]{2,3,1,0:T(2,128)S(1)}, u32[]{:S(2)}, u32[]{:S(2)}) collective-permute-start(f32[5,2,256,2]{2,3,1,0:T(2,128)S(1)} %slice.238), channel_id=1, source_target_pairs={{0,2},{1,3},{2,0},{3,1},{4,6},{5,7},{6,4},{7,5},{8,10},{9,11},{10,... | collective-permute-start | bytes 61448 | tf_op jit(solution)/shard_map/ppermute | solution.py:14
  406.7 2.1 copy-start.2
  408.5 0.9 copy-start.4
  409.5 2.5 copy-start.6
  412.9 5.9 %copy-start.7 = (f32[5,6,256,96]{2,3,1,0:T(8,128)S(1)}, f32[5,6,256,96]{2,3,1,0:T(8,128)}, u32[]{:S(2)}) copy-start(f32[5,6,256,96]{2,3,1,0:T(8,128)} %copy-done.6) | copy-start | bytes 8847364
  414.8 7.8 %collective-permute-start.4 = (f32[5,6,2,96]{3,2,1,0:T(2,128)S(1)}, f32[5,6,2,96]{3,2,1,0:T(2,128)S(1)}, u32[]{:S(2)}, u32[]{:S(2)}) collective-permute-start(f32[5,6,2,96]{3,2,1,0:T(2,128)S(1)} %copy.40), channel_id=1, source_target_pairs={{1,0},{2,1},{3,2},{0,3},{5,4},{6,5},{7,6},{4,7},{9,8},{10,9},{11,1... | collective-permute-start | bytes 69128 | tf_op jit(solution)/shard_map/ppermute | solution.py:26
  418.2 5.7 %collective-permute-start.3 = (f32[5,6,2,96]{3,2,1,0:T(2,128)S(1)}, f32[5,6,2,96]{3,2,1,0:T(2,128)S(1)}, u32[]{:S(2)}, u32[]{:S(2)}) collective-permute-start(f32[5,6,2,96]{3,2,1,0:T(2,128)S(1)} %copy.39), channel_id=1, source_target_pairs={{0,1},{1,2},{2,3},{3,0},{4,5},{5,6},{6,7},{7,4},{8,9},{9,10},{10,1... | collective-permute-start | bytes 69128 | tf_op jit(solution)/shard_map/ppermute | solution.py:24
  424.4 1.4 copy-start.1
  424.4 1.5 copy-start.3
  424.4 1.8 copy-start.5
  434.0 1.8 copy-start.8
  436.8 1.2 copy-start.9
